TPU v7x, 512 devices: a whole 4x8x8 slice. The times are simulated.
512 devices in a mesh: sta: 64 (over y, x, z_hi), win: 8 (over z_lo, core).
Axes of the slice: x: 4, y: 8, z: 8 (z_hi: 2, z_lo: 4; z = z_hi * 4 + z_lo), core: 2. Of those that a mesh axis runs over, the one named last changes fastest.
Arguments:
- spectra: float32 [16, 256, 2, 3, 1664], P('win', 'sta')
- flags: int32 [16, 256], P('win', 'sta'), may hold values 0 or 1
- owners: int32 [4], replicated, may hold values from 0 to 63, as said below
- source_slots: int32 [4, 4], replicated, may hold values from 0 to 3, as said below
Outputs:
- correlations: float32 [4, 4, 3, 256, 3, 768], P(None, None, None, 'sta')
Inputs may be any that keep to these rules, and one draw needn't show every extreme that they name: `owners`: the index of a block of 4 stations along sta. `source_slots`: distinct within a step.
All inputs are finite; a program needn't handle non-finite values. No bound on the sum of `flags` on one device may be relied on, other than what follows from the above.
Results may differ from a plain program's by a relative error of at most 0.0037.
Values sent between devices are 32-bit elements; how exact they have to be, the bound alone decides.
A program may use at most 64 MiB of HBM per device.

v0:
```python
import math

import jax
import jax.numpy as jnp
from jax import lax
from jax.sharding import PartitionSpec as P

NLAG = 768
STEPS = 4


def spread(value, axis, source):
    kept = jnp.where(lax.axis_index(axis) == source, value, 0).astype(value.dtype)
    return lax.psum(kept, axis)


def whiten(spectra):
    shape = spectra.shape
    blocks = spectra.reshape(shape[0], shape[1], 2, 3, shape[4] // 64, 64)
    power = jnp.mean(blocks * blocks, axis=(2, 3, 5), keepdims=True)
    return (blocks / jnp.sqrt(power + 1e-06)).reshape(shape)


def lag_table(bins, lags, windows):
    freq = jnp.arange(bins, dtype=jnp.int32) + 360
    shift = jnp.arange(lags, dtype=jnp.int32) - lags // 2
    phase = jnp.mod(freq[:, None] * shift[None, :], 7200).astype(jnp.float32) * (
        2.0 * math.pi / 7200.0
    )
    scale = 1.0 / math.sqrt(windows * bins)
    return jnp.concatenate([jnp.cos(phase) * scale, -jnp.sin(phase) * scale], axis=0).astype(
        jnp.bfloat16
    )


def correlate(picked, receivers, table):
    src_re = picked[:, :, 0][:, :, :, None, None, :]
    src_im = picked[:, :, 1][:, :, :, None, None, :]
    rec_re = receivers[:, :, 0][:, None, None, :, :, :]
    rec_im = receivers[:, :, 1][:, None, None, :, :, :]
    real = jnp.sum(src_re * rec_re + src_im * rec_im, axis=0)
    imag = jnp.sum(src_im * rec_re - src_re * rec_im, axis=0)
    shape = real.shape
    bins = shape[4]
    rows = jnp.concatenate([real.reshape(-1, bins), imag.reshape(-1, bins)], axis=1).astype(
        jnp.bfloat16
    )
    lagged = jnp.dot(rows, table, preferred_element_type=jnp.float32)
    return lagged.reshape(shape[0], shape[1], shape[2], shape[3], table.shape[1])


def on_device(spectra, flags, owners, source_slots):
    win_count = spectra.shape[0]
    bins = spectra.shape[4]
    weighted = whiten(spectra) * flags.astype(jnp.float32)[:, :, None, None, None]
    table = lag_table(bins, NLAG, win_count * lax.axis_size("win"))
    outputs = []
    for step in range(STEPS):
        chosen = jnp.take(weighted, source_slots[step], axis=1)
        picked = spread(chosen, "sta", owners[step])
        partial_stack = correlate(picked, weighted, table)
        partial_stack = lax.psum(partial_stack, "win")
        outputs.append(partial_stack)
    stacked = jnp.stack(outputs)
    return stacked


def solution(mesh):
    return jax.shard_map(
        on_device,
        mesh=mesh,
        in_specs=(P("win", "sta", None, None, None), P("win", "sta"), P(), P()),
        out_specs=P(None, None, None, "sta", None, None),
        check_vma=False,
    )
```

profile of v0, /device:TPU:1, one launch (start us, length us, event | category | flops | bytes accessed | tf_op | source)
XLA Modules:
  0.0 1010.7 jit_solution(12105499621488720330)
XLA Ops:
  7.2 1.5 fusion.30
  12.1 1.2 multiply_reduce_fusion
  18.6 1.2 bitcast_select_fusion
  19.8 1.2 bitcast_select_fusion.2
  21.5 23.4 %multiply_convert_fusion.1 = (bf16[1664,768]{1,0:T(8,128)(2,1)S(1)}, bf16[1664,768]{1,0:T(8,128)(2,1)}) fusion(s32[768]{0:T(1024)S(1)} %iota_add_fusion.1, s32[1664]{0:T(1024)S(1)} %iota_add_fusion), kind=kLoop, calls=%fused_computation.9 | loop fusion | flops 17891328 | bytes 5121536 | tf_op jit(solution)/shard_map/convert.12
  45.0 775.4 %all-reduce.5.cloned.1.call-done = (f32[2,4,2,3,1664]{4,2,3,0,1:T(2,128)}, f32[2,4,2,3,1664]{4,2,3,0,1:T(2,128)}, f32[2,4,2,3,1664]{4,2,3,0,1:T(2,128)}, f32[2,4,2,3,1664]{4,2,3,0,1:T(2,128)}) async-done(((f32[2,4,2,3,1664]{4,2,3,0,1:T(2,128)}, f32[2,4,2,3,1664]{4,2,3,0,1:T(2,128)}, f32[2,4,2,3,1664]{4,2,3,0,1:T(2,128)}, f32[2,4,2,3,1664]{4,2,3,0,1:T(2,128)}), (f32[2,4,2,3,1664]{4,2,3,0,1:T(2,128)}, ...) | async-done | bytes 1277968 | tf_op jit(solution)/shard_map/psum | solution.py:14
  820.3 1.4 fusion.28
  821.9 1.3 fusion.27
  824.1 14.1 %add_reduce_fusion.3 = (bf16[4,3,4,3,1664]{4,2,3,1,0:T(4,128)(2,1)S(1)}, bf16[4,3,4,3,1664]{4,2,3,1,0:T(4,128)(2,1)}, bf16[4,3,4,3,1664]{4,2,3,1,0:T(4,128)(2,1)...) fusion(f32[2,4,3,1664]{3,1,2,0:T(4,128)S(1)} %get-tuple-element, ...), kind=kLoop, calls=%fused_computation.22 | loop fusion | flops 13418496 | bytes 5431296 | tf_op jit(solution)/shard_map/reduce_sum | solution.py:41
  839.7 1.3 copy.45
  842.1 1.3 copy.51
  843.4 1.2 reshape.84
  844.6 1.3 copy.50
  845.9 1.2 reshape.83
  847.0 1.3 copy.57
  849.5 1.3 copy.56
  850.8 1.2 reshape.86
  852.0 1.3 copy.63
  853.2 1.2 reshape.90
  854.4 1.3 copy.62
  855.7 1.2 reshape.89
  856.9 3.8 fusion.5
  860.7 2.0 stack.15
  862.7 3.4 fusion.17
  866.1 2.0 stack.18
  868.1 3.8 fusion.13
  871.9 2.0 stack.17
  873.9 3.4 fusion.9
  877.4 2.0 stack.16
  879.4 120.5 %all-reduce.7.cloned.1.call-done = (f32[1,4,3,4,3,768]{5,4,3,2,1,0:T(4,128)}, f32[1,4,3,4,3,768]{5,4,3,2,1,0:T(4,128)}, f32[1,4,3,4,3,768]{5,4,3,2,1,0:T(4,128)}, f32[1,4,3,4,3,768]{5,4,3,2,1,0:T(4,128)}) async-done(((f32[1,4,3,4,3,768]{5,4,3,2,1,0:T(4,128)}, f32[1,4,3,4,3,768]{5,4,3,2,1,0:T(4,128)}, f32[1,4,3,4,3,768]{5,4,3,2,1,0:T(4,128)}, f32[1,4,3,4,3,768]{5,4,3,2,1,0:T(4,128)}), ...) | async-done | bytes 1769488 | tf_op jit(solution)/shard_map/psum | solution.py:62
  999.9 2.2 pad_maximum_fusion.1
  1002.2 1.7 copy.64
  (50 shorter events, 11.9 us)
Async XLA Ops:
  6.5 813.8 %all-reduce.5.cloned.1.call-start = ((), (), s32[]{:S(2)}) async-start(), calls=%async_computation | async-start | bytes 2555904 | tf_op jit(solution)/shard_map/psum | solution.py:14
  21.1 978.9 %all-reduce.7.cloned.1.call-start = ((), (), s32[]{:S(2)}) async-start(), calls=%async_computation.1 | async-start | bytes 4718592 | tf_op jit(solution)/shard_map/psum | solution.py:62
  820.3 3.0 copy-start.5
  820.3 3.4 copy-start.4
  856.9 5.8 copy-start.2
  856.9 5.8 copy-start.3
  868.1 5.8 copy-start
  868.1 5.8 copy-start.1
Sparse Core Ops, SparseCore 0:
  21.2 799.0 all-reduce.4
  879.5 120.3 all-reduce.6
where the time goes:
time: 1010 us
  waiting for transfers between devices  896 us (89%)
  other arithmetic  46.3 us (5%)
  local copies, waits for them, and re-layouts  37.7 us (4%)
  between operations  16.2 us (2%)
  matrix products  14.4 us (1%)
    psum x1, waiting for transfers between devices, spread(): return lax.psum(kept, axis)  775 us
    psum x1, waiting for transfers between devices, on_device(): partial_stack = lax.psum(partial_stack, 'win')  121 us
    another operation x1, other arithmetic  23.4 us
  transfers between devices with their start and end apart: 2, of which 2 were waited for; matrix products, arithmetic and copies ran while one was open for 2% of the time, Pallas kernels for 0%

commit v1 on v0

--- a/solution.py
+++ b/solution.py
@@ -3,15 +3,25 @@
 import jax
 import jax.numpy as jnp
 from jax import lax
+from jax.sharding import Mesh
 from jax.sharding import PartitionSpec as P
 
 NLAG = 768
 STEPS = 4
+STA = ("y", "x", "zh")
+WIN = ("zl", "c")
 
 
-def spread(value, axis, source):
-    kept = jnp.where(lax.axis_index(axis) == source, value, 0).astype(value.dtype)
-    return lax.psum(kept, axis)
+def fine_mesh(mesh):
+    devs = mesh.devices
+    n_sta, n_win = devs.shape
+    col = devs[:, 0]
+    ny = len({d.coords[1] for d in col})
+    nx = len({d.coords[0] for d in col})
+    nzh = n_sta // (ny * nx)
+    nc = len({d.core_on_chip for d in devs[0, :]})
+    nzl = n_win // nc
+    return Mesh(devs.reshape(ny, nx, nzh, nzl, nc), STA + WIN)
 
 
 def whiten(spectra):
@@ -53,23 +63,31 @@
     win_count = spectra.shape[0]
     bins = spectra.shape[4]
     weighted = whiten(spectra) * flags.astype(jnp.float32)[:, :, None, None, None]
-    table = lag_table(bins, NLAG, win_count * lax.axis_size("win"))
+    n_win = lax.axis_size(WIN)
+    table = lag_table(bins, NLAG, win_count * n_win)
+    me = lax.axis_index(STA)
+    chosen = []
+    for step in range(STEPS):
+        block = jnp.take(weighted, source_slots[step], axis=1)
+        chosen.append(jnp.where(me == owners[step], block, 0.0))
+    picked_all = jnp.stack(chosen)
+    for axis in ("zh", "x", "y"):
+        picked_all = lax.psum(picked_all, axis)
     outputs = []
     for step in range(STEPS):
-        chosen = jnp.take(weighted, source_slots[step], axis=1)
-        picked = spread(chosen, "sta", owners[step])
-        partial_stack = correlate(picked, weighted, table)
-        partial_stack = lax.psum(partial_stack, "win")
-        outputs.append(partial_stack)
+        outputs.append(correlate(picked_all[step], weighted, table))
     stacked = jnp.stack(outputs)
+    for axis in ("c", "zl"):
+        stacked = lax.psum(stacked, axis)
     return stacked
 
 
 def solution(mesh):
+    fine = fine_mesh(mesh)
     return jax.shard_map(
         on_device,
-        mesh=mesh,
-        in_specs=(P("win", "sta", None, None, None), P("win", "sta"), P(), P()),
-        out_specs=P(None, None, None, "sta", None, None),
+        mesh=fine,
+        in_specs=(P(WIN, STA, None, None, None), P(WIN, STA), P(), P()),
+        out_specs=P(None, None, None, STA, None, None),
         check_vma=False,
     )

time: 1010 us -> 489 us (0.48)
  waiting for transfers between devices: 896 us -> 372 us
    psum x2 -> x5, waiting for transfers between devices: 896 us -> 372 us  [the longest x3 215 us: on_device(): picked_all = lax.psum(picked_all, axis)]
    another operation x1 -> x4, other arithmetic: 23.4 us -> 25.9 us
  transfers between devices with their start and end apart: 2 -> 5, of which waited for: 2 -> 5; matrix products, arithmetic and copies ran while one was open for 2% -> 5% of each run, Pallas kernels for 0% -> 0%
where the time goes in v1:
time: 489 us; the launch traced here: 488 us
  waiting for transfers between devices  372 us (76%)
  other arithmetic  47.4 us (10%)
  local copies, waits for them, and re-layouts  36.9 us (8%)
  between operations  16 us (3%)
  matrix products  14.9 us (3%)
    psum x3, waiting for transfers between devices, on_device(): picked_all = lax.psum(picked_all, axis)  215 us
    psum x2, waiting for transfers between devices, on_device(): stacked = lax.psum(stacked, axis)  157 us
    another operation x1, other arithmetic  23.4 us
    dot_general x4, matrix products, correlate(): lagged = jnp.dot(rows, table, preferred_element_type=jnp.float32)  14.9 us
    reduce_sum x1, other arithmetic, correlate(): real = jnp.sum(src_re * rec_re + src_im * rec_im, axis=0)  14.1 us
  transfers between devices with their start and end apart: 5, of which 5 were waited for; matrix products, arithmetic and copies ran while one was open for 5% of the time, Pallas kernels for 0%

profile of v1, /device:TPU:1, one launch (start us, length us, event | category | flops | bytes accessed | tf_op | source)
XLA Modules:
  0.0 487.6 jit_solution(13169623041716736333)
XLA Ops:
  7.2 1.5 fusion.34
  12.1 1.2 multiply_reduce_fusion
  19.4 1.6 pad_maximum_fusion.2
  21.1 100.1 %all-reduce.6.cloned.1.call-done = f32[4,2,4,2,3,1664]{5,3,4,1,2,0:T(2,128)} async-done(((f32[4,2,4,2,3,1664]{5,3,4,1,2,0:T(2,128)}), f32[4,2,4,2,3,1664]{5,3,4,1,2,0:T(2,128)}) %all-reduce.6.cloned.1.call-update) | async-done | bytes 1277968 | tf_op jit(solution)/shard_map/psum | solution.py:75
  121.5 55.5 %all-reduce.8.cloned.1.call-done = f32[4,2,4,2,3,1664]{5,3,4,1,2,0:T(2,128)} async-done(((f32[4,2,4,2,3,1664]{5,3,4,1,2,0:T(2,128)}), f32[4,2,4,2,3,1664]{5,3,4,1,2,0:T(2,128)}) %all-reduce.8.cloned.1.call-update) | async-done | bytes 1277968 | tf_op jit(solution)/shard_map/psum | solution.py:75
  177.2 23.4 %multiply_convert_fusion.1 = (bf16[1664,768]{1,0:T(8,128)(2,1)S(1)}, bf16[1664,768]{1,0:T(8,128)(2,1)}) fusion(s32[768]{0:T(1024)S(1)} %iota_add_fusion.1, s32[1664]{0:T(1024)S(1)} %iota_add_fusion), kind=kLoop, calls=%fused_computation.9 | loop fusion | flops 17891328 | bytes 5121536 | tf_op jit(solution)/shard_map/convert.12
  200.7 59.8 %all-reduce.10.cloned.1.call-done = f32[4,2,4,2,3,1664]{5,3,4,1,2,0:T(2,128)} async-done(((f32[4,2,4,2,3,1664]{5,3,4,1,2,0:T(2,128)}), f32[4,2,4,2,3,1664]{5,3,4,1,2,0:T(2,128)}) %all-reduce.10.cloned.1.call-update) | async-done | bytes 1277968 | tf_op jit(solution)/shard_map/psum | solution.py:75
  260.5 1.4 slice_bitcast_fusion
  263.4 14.1 %add_reduce_fusion.3 = (bf16[4,3,4,3,1664]{4,2,3,1,0:T(4,128)(2,1)S(1)}, bf16[4,3,4,3,1664]{4,2,3,1,0:T(4,128)(2,1)}, bf16[4,3,4,3,1664]{4,2,3,1,0:T(4,128)(2,1)...) fusion(f32[2,4,3,1664]{3,1,2,0:T(4,128)S(1)} %get-tuple-element, ...), kind=kLoop, calls=%fused_computation.22 | loop fusion | flops 13418496 | bytes 5431296 | tf_op jit(solution)/shard_map/reduce_sum | solution.py:51
  277.7 1.2 reshape.68
  278.9 1.3 copy.45
  280.2 1.2 reshape.69
  281.4 1.3 copy.51
  282.7 1.2 reshape.71
  283.8 1.3 copy.50
  286.3 1.3 copy.57
  288.7 1.3 copy.56
  291.2 1.3 copy.63
  293.6 1.3 copy.62
  294.9 1.2 reshape.74
  296.1 3.7 fusion.5
  299.8 1.2 stack_reshape.12
  301.0 3.7 fusion.17
  304.8 2.0 stack_reshape.15
  306.8 3.7 fusion.13
  310.5 2.0 stack_reshape.14
  312.5 3.7 fusion.9
  316.2 1.2 stack_reshape.13
  317.4 3.4 pad_maximum_fusion.1
  321.0 42.1 %all-reduce.12.cloned.1.call-done = f32[4,4,3,4,3,768]{5,4,3,2,1,0:T(4,128)} async-done(((f32[4,4,3,4,3,768]{5,4,3,2,1,0:T(4,128)}), f32[4,4,3,4,3,768]{5,4,3,2,1,0:T(4,128)}) %all-reduce.12.cloned.1.call-update) | async-done | bytes 1769488 | tf_op jit(solution)/shard_map/psum | solution.py:81
  363.1 114.7 %all-reduce.14.cloned.1.call-done = f32[4,4,3,4,3,768]{5,4,3,2,1,0:T(4,128)} async-done(((f32[4,4,3,4,3,768]{5,4,3,2,1,0:T(4,128)}), f32[4,4,3,4,3,768]{5,4,3,2,1,0:T(4,128)}) %all-reduce.14.cloned.1.call-update) | async-done | bytes 1769488 | tf_op jit(solution)/shard_map/psum | solution.py:81
  477.8 3.3 copy.64
  (49 shorter events, 14.5 us)
Async XLA Ops:
  6.5 114.6 %all-reduce.6.cloned.1.call-start = ((), (), s32[]{:S(2)}) async-start(), calls=%async_computation | async-start | bytes 2555904 | tf_op jit(solution)/shard_map/psum | solution.py:75
  21.0 156.0 %all-reduce.8.cloned.1.call-start = ((), (), s32[]{:S(2)}) async-start(), calls=%async_computation.1 | async-start | bytes 2555904 | tf_op jit(solution)/shard_map/psum | solution.py:75
  121.2 139.3 %all-reduce.10.cloned.1.call-start = ((), (), s32[]{:S(2)}) async-start(), calls=%async_computation.2 | async-start | bytes 2555904 | tf_op jit(solution)/shard_map/psum | solution.py:75
  177.1 186.0 %all-reduce.12.cloned.1.call-start = ((), (), s32[]{:S(2)}) async-start(), calls=%async_computation.3 | async-start | bytes 4718592 | tf_op jit(solution)/shard_map/psum | solution.py:81
  320.9 156.9 %all-reduce.14.cloned.1.call-start = ((), (), s32[]{:S(2)}) async-start(), calls=%async_computation.4 | async-start | bytes 4718592 | tf_op jit(solution)/shard_map/psum | solution.py:81
Sparse Core Ops, SparseCore 0:
  21.2 99.9 all-reduce.5
  123.6 53.4 all-reduce.7
  179.5 80.9 all-reduce.9
  321.0 41.9 all-reduce.11
  365.8 111.9 all-reduce.13
